TPU v7x, 128 devices: a whole 4x4x4 slice. The times are simulated.
128 devices in a mesh: dp: 16 (over x_lo, y, core), tensor: 8 (over x_hi, z).
Axes of the slice: x: 4 (x_hi: 2, x_lo: 2; x = x_hi * 2 + x_lo), y: 4, z: 4, core: 2. Of those that a mesh axis runs over, the one named last changes fastest.
Arguments:
- block_input: bfloat16 [32768, 768], P(('dp', 'tensor')), may hold values from -6 to 6
- w_value: bfloat16 [768, 768], replicated, may hold values from -0.21875 to 0.21875
- b_value: bfloat16 [768], replicated, may hold values from -2 to 2
- conv_kernel: bfloat16 [65, 768], replicated, may hold values from -0.75 to 0.75
- w_out: bfloat16 [768, 768], replicated, may hold values from -0.21875 to 0.21875
- b_out: bfloat16 [768], replicated, may hold values from -2 to 2
- gain_attn: bfloat16 [768], replicated, may hold values from 0.5 to 1.5
- shift_attn: bfloat16 [768], replicated, may hold values from -2 to 2
- w_up: bfloat16 [768, 3072], P(None, 'tensor'), may hold values from -0.21875 to 0.21875
- b_up: bfloat16 [3072], P('tensor'), may hold values from -2 to 2
- w_down: bfloat16 [3072, 768], P('tensor'), may hold values from -0.109375 to 0.109375
- b_down: bfloat16 [768], replicated, may hold values from -2 to 2
- gain_ffn: bfloat16 [768], replicated, may hold values from 0.5 to 1.5
- shift_ffn: bfloat16 [768], replicated, may hold values from -2 to 2
- query_codes: int32 [32768, 384], P(('dp', 'tensor')), may hold values from 0 to 255
- key_codes: int32 [32768, 384], P(('dp', 'tensor')), may hold values from 0 to 255
- key_live: int32 [32768], P(('dp', 'tensor')), may hold values 0 or 1
- seq_lengths: int32 [128, 4], P(('dp', 'tensor')), may hold values from 1 to 128, 256 in all within a row
- out_grad: bfloat16 [32768, 768], P(('dp', 'tensor')), may hold values from -6 to 6
Outputs:
- block_output: bfloat16 [32768, 768], P(('dp', 'tensor'))
- input_grad: float32 [32768, 768], P(('dp', 'tensor'))
- grad_w_value: float32 [768, 768], replicated
- grad_b_value: float32 [768], replicated
- grad_conv_kernel: float32 [65, 768], replicated
- grad_w_out: float32 [768, 768], replicated
- grad_b_out: float32 [768], replicated
- grad_gain_attn: float32 [768], replicated
- grad_shift_attn: float32 [768], replicated
- grad_w_up: float32 [768, 3072], P(None, 'tensor')
- grad_b_up: float32 [3072], P('tensor')
- grad_w_down: float32 [3072, 768], P('tensor')
- grad_b_down: float32 [768], replicated
- grad_gain_ffn: float32 [768], replicated
- grad_shift_ffn: float32 [768], replicated
Inputs may be any that keep to these rules, and one draw needn't show every extreme that they name: `seq_lengths`: each item's lengths sum to 256; the longest is 128. `key_live`: 1 marks a live key, 0 a padded one. `query_codes`: column h * 32 + s holds head h's code in hash set s. `key_codes`: column h * 32 + s holds head h's code in hash set s.
All inputs are finite; a program needn't handle non-finite values. No bound on the sum of `key_live` on one device may be relied on, other than what follows from the above.
Results may differ from a plain program's by a relative error of at most 0.02.
Values may be sent and summed in bfloat16 or wider, within the bound.
No kernel may reach another device: no remote copies, remote signals or barrier semaphores. Data moves between devices by JAX's collectives and lax.ppermute only.
A program may use at most 128 MiB of HBM per device.

v0:
```python
from functools import partial
import jax
import jax.numpy as jnp
from jax import lax
from jax.sharding import PartitionSpec as P

HEADS = 12
SETS = 32
BUCKETS = 256


def dot_last(former, latter):
    return lax.dot_general(
        former, latter, (((1,), (1,)), ((), ())), preferred_element_type=jnp.float32
    )


def dot_first(former, latter):
    return lax.dot_general(
        former, latter, (((0,), (0,)), ((), ())), preferred_element_type=jnp.float32
    )


def layer_norm(residual, gain_vec, shift_vec):
    average = jnp.mean(residual, axis=-1, keepdims=True)
    centred = residual - average
    variance = jnp.mean(centred * centred, axis=-1, keepdims=True)
    return centred * lax.rsqrt(variance + 1e-05) * gain_vec + shift_vec


def head_norm(mixed, head_count, head_dim):
    grouped = mixed.reshape(mixed.shape[0], head_count, head_dim)
    scaling = lax.rsqrt(jnp.mean(grouped * grouped, axis=-1, keepdims=True) + 1e-06)
    return (grouped * scaling).reshape(mixed.shape)


def gelu_exact(pre_act):
    return jax.nn.gelu(pre_act, approximate=False)


def depth_conv(values, kernel, segment):
    taps = kernel.shape[0]
    margin = taps // 2
    length = values.shape[0]
    padded = jnp.pad(values, ((margin, margin), (0, 0)))
    seg_padded = jnp.pad(segment, (margin, margin), constant_values=-1)
    running = jnp.zeros_like(values)
    for offset in range(taps):
        joined = (seg_padded[offset : offset + length] == segment).astype(jnp.float32)[:, None]
        running = running + padded[offset : offset + length] * joined * kernel[offset][None, :]
    return running


def conv_back(grad_out, values, kernel, segment):
    taps = kernel.shape[0]
    margin = taps // 2
    length = values.shape[0]
    padded = jnp.pad(values, ((margin, margin), (0, 0)))
    grad_padded = jnp.pad(grad_out, ((margin, margin), (0, 0)))
    seg_padded = jnp.pad(segment, (margin, margin), constant_values=-1)
    value_grad = jnp.zeros_like(values)
    tap_rows = []
    for offset in range(taps):
        joined = (seg_padded[offset : offset + length] == segment).astype(jnp.float32)[:, None]
        tap_rows.append(jnp.sum(grad_out * joined * padded[offset : offset + length], axis=0))
        mirror = 2 * margin - offset
        back_joined = (seg_padded[mirror : mirror + length] == segment).astype(jnp.float32)[:, None]
        value_grad = (
            value_grad
            + grad_padded[mirror : mirror + length] * back_joined * kernel[offset][None, :]
        )
    return (value_grad, jnp.stack(tap_rows, axis=0))


def body(
    block_input,
    w_value,
    b_value,
    conv_kernel,
    w_out,
    b_out,
    gain_attn,
    shift_attn,
    w_up,
    b_up,
    w_down,
    b_down,
    gain_ffn,
    shift_ffn,
    query_codes,
    key_codes,
    key_live,
    seq_lengths,
    out_grad,
):
    length = block_input.shape[0]
    model_width = block_input.shape[1]
    head_dim = model_width // HEADS
    live_keys = key_live.astype(jnp.float32)[:, None]
    seq_ends = jnp.cumsum(seq_lengths[0], dtype=jnp.int32)
    positions = jnp.arange(length, dtype=jnp.int32)
    segment = jnp.sum(
        (seq_ends[None, :] <= positions[:, None]).astype(jnp.int32), axis=1, dtype=jnp.int32
    )
    query_heads = query_codes.reshape(length, HEADS, SETS).transpose(1, 0, 2)
    key_heads = key_codes.reshape(length, HEADS, SETS).transpose(1, 0, 2)
    joined = (segment[:, None] == segment[None, :]).astype(jnp.float32)
    bucket_ids = jnp.arange(BUCKETS, dtype=jnp.int32)

    def head_counts(pair):
        query_set, key_set = pair
        query_hot = (
            (query_set[:, :, None] == bucket_ids[None, None, :])
            .astype(jnp.bfloat16)
            .reshape(length, SETS * BUCKETS)
        )
        key_hot = (
            (key_set[:, :, None] == bucket_ids[None, None, :])
            .astype(jnp.bfloat16)
            .reshape(length, SETS * BUCKETS)
        )
        counts = dot_last(query_hot, key_hot)
        return (counts * joined / SETS).astype(jnp.bfloat16)

    collide = lax.map(head_counts, (query_heads, key_heads))
    kernel_f = conv_kernel.astype(jnp.float32)
    value_pre = jnp.dot(block_input, w_value, preferred_element_type=jnp.float32) + b_value.astype(
        jnp.float32
    )
    values = value_pre.astype(jnp.bfloat16)
    masked = values.astype(jnp.float32) * live_keys
    masked_low = masked.astype(jnp.bfloat16)
    mixed = jnp.einsum(
        "hij,jhd->ihd",
        collide,
        masked_low.reshape(length, HEADS, head_dim),
        preferred_element_type=jnp.float32,
    ).reshape(length, model_width)
    normed, norm_back = jax.vjp(partial(head_norm, head_count=HEADS, head_dim=head_dim), mixed)
    context = (normed + depth_conv(masked, kernel_f, segment)).astype(jnp.bfloat16)
    attended = jnp.dot(context, w_out, preferred_element_type=jnp.float32) + b_out.astype(
        jnp.float32
    )
    first, first_back = jax.vjp(
        layer_norm,
        block_input.astype(jnp.float32) + attended,
        gain_attn.astype(jnp.float32),
        shift_attn.astype(jnp.float32),
    )
    first_low = first.astype(jnp.bfloat16)
    gathered = lax.all_gather(first_low, "tensor", axis=0, tiled=True)
    upper = jnp.dot(gathered, w_up, preferred_element_type=jnp.float32) + b_up.astype(jnp.float32)
    active_f, gelu_back = jax.vjp(gelu_exact, upper)
    active = active_f.astype(jnp.bfloat16)
    branch = lax.psum_scatter(
        jnp.dot(active, w_down, preferred_element_type=jnp.float32).astype(jnp.bfloat16),
        "tensor",
        scatter_dimension=0,
        tiled=True,
    ).astype(jnp.float32) + b_down.astype(jnp.float32)
    block_output, second_back = jax.vjp(
        layer_norm, first + branch, gain_ffn.astype(jnp.float32), shift_ffn.astype(jnp.float32)
    )
    grad_second, grad_gain_ffn, grad_shift_ffn = second_back(out_grad.astype(jnp.float32))
    branch_grad = grad_second.astype(jnp.bfloat16)
    grad_b_down = jnp.sum(branch_grad.astype(jnp.float32), axis=0)
    grad_rows_all = lax.all_gather(branch_grad, "tensor", axis=0, tiled=True)
    active_grad = dot_last(grad_rows_all, w_down)
    grad_w_down = dot_first(active, grad_rows_all)
    upper_grad = gelu_back(active_grad)[0].astype(jnp.bfloat16)
    grad_w_up = dot_first(gathered, upper_grad)
    grad_b_up = jnp.sum(upper_grad.astype(jnp.float32), axis=0)
    first_grad_ffn = lax.psum_scatter(
        dot_last(upper_grad, w_up).astype(jnp.bfloat16), "tensor", scatter_dimension=0, tiled=True
    ).astype(jnp.float32)
    first_grad = grad_second + first_grad_ffn
    resid_grad, grad_gain_attn, grad_shift_attn = first_back(first_grad)
    attended_grad = resid_grad.astype(jnp.bfloat16)
    grad_b_out = jnp.sum(attended_grad.astype(jnp.float32), axis=0)
    grad_w_out = dot_first(context, attended_grad)
    context_grad = dot_last(attended_grad, w_out)
    mixed_grad = norm_back(context_grad)[0].astype(jnp.bfloat16)
    conv_value_grad, grad_kernel = conv_back(context_grad, masked, kernel_f, segment)
    masked_att = jnp.einsum(
        "hij,ihd->jhd",
        collide,
        mixed_grad.reshape(length, HEADS, head_dim),
        preferred_element_type=jnp.float32,
    ).reshape(length, model_width)
    value_grad = ((masked_att + conv_value_grad) * live_keys).astype(jnp.bfloat16)
    grad_b_value = jnp.sum(value_grad.astype(jnp.float32), axis=0)
    grad_w_value = dot_first(block_input, value_grad)
    input_grad = resid_grad + dot_last(value_grad, w_value)
    grad_w_up, grad_w_down, grad_b_up = (
        lax.psum(grad_w_up.astype(jnp.bfloat16), "dp").astype(jnp.float32),
        lax.psum(grad_w_down.astype(jnp.bfloat16), "dp").astype(jnp.float32),
        lax.psum(grad_b_up.astype(jnp.bfloat16), "dp").astype(jnp.float32),
    )
    (
        grad_w_value,
        grad_b_value,
        grad_kernel,
        grad_w_out,
        grad_b_out,
        grad_gain_attn,
        grad_shift_attn,
        grad_b_down,
        grad_gain_ffn,
        grad_shift_ffn,
    ) = lax.psum(
        (
            grad_w_value,
            grad_b_value,
            grad_kernel,
            grad_w_out,
            grad_b_out,
            grad_gain_attn,
            grad_shift_attn,
            grad_b_down,
            grad_gain_ffn,
            grad_shift_ffn,
        ),
        ("dp", "tensor"),
    )
    return (
        block_output.astype(jnp.bfloat16),
        input_grad,
        grad_w_value,
        grad_b_value,
        grad_kernel,
        grad_w_out,
        grad_b_out,
        grad_gain_attn,
        grad_shift_attn,
        grad_w_up,
        grad_b_up,
        grad_w_down,
        grad_b_down,
        grad_gain_ffn,
        grad_shift_ffn,
    )


def solution(mesh):
    return jax.shard_map(
        body,
        mesh=mesh,
        in_specs=(
            P(("dp", "tensor"), None),
            P(),
            P(),
            P(),
            P(),
            P(),
            P(),
            P(),
            P(None, "tensor"),
            P("tensor"),
            P("tensor", None),
            P(),
            P(),
            P(),
            P(("dp", "tensor"), None),
            P(("dp", "tensor"), None),
            P(("dp", "tensor")),
            P(("dp", "tensor"), None),
            P(("dp", "tensor"), None),
        ),
        out_specs=(
            P(("dp", "tensor"), None),
            P(("dp", "tensor"), None),
            P(),
            P(),
            P(),
            P(),
            P(),
            P(),
            P(),
            P(None, "tensor"),
            P("tensor"),
            P("tensor", None),
            P(),
            P(),
            P(),
        ),
        check_vma=False,
    )
```

profile of v0, /device:TPU:1, one launch (start us, length us, event | category | flops | bytes accessed | tf_op | source)
XLA Modules:
  0.0 701.4 jit_solution(10940862884612107198)
XLA Ops:
  17.3 43.1 %while.12 = (s32[]{:T(128)}, bf16[12,256,256]{2,1,0:T(8,128)(2,1)}, s32[12,256,32]{1,2,0:T(8,128)S(1)}, s32[12,256,32]{1,2,0:T(8,128)S(1)}, s32[256]{0:T(256)S(1)}, /*index=5*/s32[]{:T(128)}) while((s32[]{:T(128)}, bf16[12,256,256]{2,1,0:T(8,128)(2,1)}, s32[12,256,32]{1,2,0:T(8,128)S(1)}, s32[12,256,32]{1,2,0:T(8,128)S(1)}, ...), condition=%wide.region_3.4_spmd.clone.clone, body=%wide.region_2.3_spmd.clone.clone.sunk | while | flops 1078198272 | bytes 330313 | solution.py:125
  17.4 3.6 fusion.266
  21.0 3.6 fusion.266
  24.6 3.6 fusion.266
  28.1 3.6 fusion.266
  35.3 3.6 fusion.266
  42.5 3.6 fusion.266
  46.1 3.6 fusion.266
  53.3 3.6 fusion.266
  66.3 11.6 %add_convert_fusion.2 = bf16[256,768]{1,0:T(8,128)(2,1)S(1)} fusion(f32[256,768]{1,0:T(8,128)S(1)} %copy.51, f32[256,768]{1,0:T(8,128)S(1)} %get-tuple-element.368, f32[768]{0:T(1024)} %get-tuple-element.198, f32[256]{0:T(256)} %get-tuple-element.366, f32[768]{0:T(1024)} %get-tuple-element.199, f32[256]{0:T(256)} %get-tuple-element.365, ...), kind=kLoop, calls=%fused_computation.456 | loop fusion | flops 38338560 | bytes 2231296 | tf_op jit(solution)/shard_map/convert_element_type | solution.py:140
  83.6 11.4 %reduce-scatter.3.cloned.1.call-start = ((), (), s32[]{:S(2)}) async-start(), calls=%async_computation.3 | async-start | bytes 3538944 | tf_op jit(solution)/shard_map/reduce_scatter | solution.py:155
  96.2 53.2 %all-gather.3.cloned.1.call-done = bf16[2048,768]{1,0:T(8,128)(2,1)} async-done(((bf16[256,768]{1,0:T(8,128)(2,1)}), bf16[2048,768]{1,0:T(8,128)(2,1)}) %all-gather.3.cloned.1.call-update) | async-done | bytes 3145744 | tf_op jit(solution)/shard_map/all_gather | solution.py:151
  149.4 11.6 %multiply_convert_fusion = (bf16[2048,384]{1,0:T(8,128)(2,1)S(1)}, f32[2048,384]{1,0:T(8,128)}, f32[2048,384]{1,0:T(8,128)}) fusion(f32[384]{0:T(512)} %convert_element_type.529, bf16[2048,768]{1,0:T(8,128)(2,1)} %all-gather.3.cloned.1.call-done, bf16[768,384]{1,0:T(8,128)(2,1)} %param.29), kind=kOutput, calls=%fused_computation.148 | convolution fusion | flops 1259864064 | bytes 11601408 | tf_op jit(solution)/shard_map/dot_general | solution.py:152
  169.5 72.7 %reduce-scatter.3.cloned.1.call-done = bf16[256,768]{1,0:T(8,128)(2,1)} async-done(((bf16[2048,768]{1,0:T(8,128)(2,1)}), bf16[256,768]{1,0:T(8,128)(2,1)}) %reduce-scatter.3.cloned.1.call-update) | async-done | bytes 393232 | tf_op jit(solution)/shard_map/reduce_scatter | solution.py:155
  249.4 62.5 %all-gather.5.cloned.1.call-done = bf16[2048,768]{1,0:T(8,128)(2,1)} async-done(((bf16[256,768]{1,0:T(8,128)(2,1)}), bf16[2048,768]{1,0:T(8,128)(2,1)}) %all-gather.5.cloned.1.call-update) | async-done | bytes 3145744 | tf_op jit(solution)/shard_map/all_gather | solution.py:167
  311.9 7.3 %fusion.230 = (bf16[384]{0:T(512)(128)(2,1)}, bf16[2048,384]{1,0:T(8,128)(2,1)S(1)}) fusion(f32[2048,384]{1,0:T(8,128)} %get-tuple-element.299, f32[2048,384]{1,0:T(8,128)} %get-tuple-element.373, bf16[2048,768]{1,0:T(8,128)(2,1)} %all-gather.5.cloned.1.call-done, bf16[384,768]{1,0:T(8,128)(2,1)} %param.31), kind=kOutput, calls=%fused_computation.674 | convolution fusion | flops 1219755648 | bytes 11600640 | tf_op jit(solution)/shard_map/dot_general | solution.py:13
  324.0 4.8 convolution_convert_fusion.2
  331.5 69.1 %reduce-scatter.5.cloned.1.call-done = bf16[256,768]{1,0:T(8,128)(2,1)} async-done(((bf16[2048,768]{1,0:T(8,128)(2,1)}), bf16[256,768]{1,0:T(8,128)(2,1)}) %reduce-scatter.5.cloned.1.call-update) | async-done | bytes 393232 | tf_op jit(solution)/shard_map/reduce_scatter | solution.py:173
  451.9 5.8 stack.263
  457.7 11.7 %convert_reduce_fusion.3 = (f32[768]{0:T(1024)S(1)}, bf16[256,768]{1,0:T(8,128)(2,1)S(1)}) fusion(f32[256]{0:T(256)} %copy-done.110, f32[256,768]{1,0:T(8,128)S(1)} %copy.53, f32[768]{0:T(1024)} %get-tuple-element.198, f32[256]{0:T(256)} %get-tuple-element.303, f32[768]{0:T(1024)} %get-tuple-element.199, f32[256]{0:T(256)} %get-tuple-element.321, ...), kind=kLoop, calls=%fused_computation.446 | loop fusion | flops 38927616 | bytes 2235392 | tf_op jit(solution)/shard_map/reduce_sum | solution.py:191
  472.0 28.5 %psum.99 = bf16[384]{0:T(512)(128)(2,1)S(1)} all-reduce(bf16[384]{0:T(512)(128)(2,1)S(1)} %copy-done.120), channel_id=1, replica_groups=mesh['dp'=16,'tensor'=8] {'dp'}, use_global_device_ids=true, to_apply=%region_94.95 | all-reduce | flops 384 | bytes 1536 | tf_op jit(solution)/shard_map/psum | solution.py:197
  501.1 22.6 %all-reduce.11.cloned.1.call-done = (bf16[768,384]{1,0:T(8,128)(2,1)}, bf16[384,768]{1,0:T(8,128)(2,1)}) async-done(((bf16[768,384]{1,0:T(8,128)(2,1)}, bf16[384,768]{1,0:T(8,128)(2,1)}), (bf16[768,384]{1,0:T(8,128)(2,1)}, bf16[384,768]{1,0:T(8,128)(2,1)})) %all-reduce.11.cloned.1.call-update) | async-done | bytes 1179664 | tf_op jit(solution)/shard_map/psum | solution.py:195
  528.0 68.4 %all-reduce.3 = (f32[768]{0:T(1024)}, f32[768]{0:T(1024)}, f32[768]{0:T(1024)}, f32[768]{0:T(1024)}, f32[768]{0:T(1024)}, /*index=5*/f32[768]{0:T(1024)}, f32[768]{0:T(1024)}) all-reduce(f32[768]{0:T(1024)S(1)} %get-tuple-element.290, f32[768]{0:T(1024)S(1)} %copy-done.37, ...), channel_id=1, replica_groups=mesh['dp'=16,'tensor'=8] {'dp','tensor'}, use_global_device_ids=true, to_apply=%region_18.19 | all-reduce | flops 5376 | bytes 43008 | tf_op jit(solution)/shard_map/psum | solution.py:210
  597.9 89.3 %all-reduce.9.cloned.1.call-done = (f32[768,768]{0,1:T(8,128)}, f32[65,768]{1,0:T(8,128)}, f32[768,768]{1,0:T(8,128)}) async-done(((f32[768,768]{0,1:T(8,128)}, f32[65,768]{1,0:T(8,128)}, f32[768,768]{1,0:T(8,128)}), (f32[768,768]{0,1:T(8,128)}, f32[65,768]{1,0:T(8,128)}, f32[768,768]{1,0:T(8,128)})) %all-reduce.9.cloned.1.call-update) | async-done | bytes 4918288 | tf_op jit(solution)/shard_map/psum | solution.py:210
  (413 shorter events, 125.8 us)
Async XLA Ops:
  7.2 53.3 %copy-start = (bf16[768,768]{1,0:T(8,128)(2,1)S(1)}, bf16[768,768]{1,0:T(8,128)(2,1)}, u32[]{:S(2)}) copy-start(bf16[768,768]{1,0:T(8,128)(2,1)} %param.22) | copy-start | bytes 3538948
  7.2 142.2 %all-gather.3.cloned.1.call-start = ((), (), s32[]{:S(2)}) async-start(), calls=%async_computation.2 | async-start | bytes 3538944 | tf_op jit(solution)/shard_map/all_gather | solution.py:151
  17.3 43.1 %copy-start.119 = (s32[256]{0:T(256)S(1)}, s32[256]{0:T(256)}, u32[]{:S(2)}) copy-start(s32[256]{0:T(256)} %param.37) | copy-start | bytes 3076
  17.3 43.1 %copy-start.116 = (bf16[768]{0:T(1024)(128)(2,1)S(1)}, bf16[768]{0:T(1024)(128)(2,1)}, u32[]{:S(2)}) copy-start(bf16[768]{0:T(1024)(128)(2,1)} %param.23) | copy-start | bytes 4612
  17.3 43.1 %copy-start.6 = (bf16[256,768]{1,0:T(8,128)(2,1)S(1)}, bf16[256,768]{1,0:T(8,128)(2,1)}, u32[]{:S(2)}) copy-start(bf16[256,768]{1,0:T(8,128)(2,1)} %param.21) | copy-start | bytes 1179652
  83.6 158.7 %reduce-scatter.3.cloned.1.call-start = ((), (), s32[]{:S(2)}) async-start(), calls=%async_computation.3 | async-start | bytes 3538944 | tf_op jit(solution)/shard_map/reduce_scatter | solution.py:155
  165.6 146.3 %all-gather.5.cloned.1.call-start = ((), (), s32[]{:S(2)}) async-start(), calls=%async_computation.4 | async-start | bytes 3538944 | tf_op jit(solution)/shard_map/all_gather | solution.py:167
  249.3 151.3 %reduce-scatter.5.cloned.1.call-start = ((), (), s32[]{:S(2)}) async-start(), calls=%async_computation.5 | async-start | bytes 3538944 | tf_op jit(solution)/shard_map/reduce_scatter | solution.py:173
  323.9 199.8 %all-reduce.11.cloned.1.call-start = ((), (), s32[]{:S(2)}) async-start(), calls=%async_computation.7 | async-start | bytes 2359296 | tf_op jit(solution)/shard_map/psum | solution.py:195
  331.4 355.7 %all-reduce.9.cloned.1.call-start = ((), (), s32[]{:S(2)}) async-start(), calls=%async_computation.6 | async-start | bytes 9879552 | tf_op jit(solution)/shard_map/psum | solution.py:210
  429.2 21.2 %copy-start.42 = (f32[768]{0:T(1024)S(1)}, f32[768]{0:T(1024)}, u32[]{:S(2)}) copy-start(f32[768]{0:T(1024)} %get-tuple-element.186) | copy-start | bytes 9220
  429.2 21.2 %copy-start.41 = (f32[768]{0:T(1024)S(1)}, f32[768]{0:T(1024)}, u32[]{:S(2)}) copy-start(f32[768]{0:T(1024)} %get-tuple-element.185) | copy-start | bytes 9220
  429.2 21.3 %copy-start.40 = (f32[768]{0:T(1024)S(1)}, f32[768]{0:T(1024)}, u32[]{:S(2)}) copy-start(f32[768]{0:T(1024)} %get-tuple-element.184) | copy-start | bytes 9220
  429.2 21.3 %copy-start.39 = (f32[768]{0:T(1024)S(1)}, f32[768]{0:T(1024)}, u32[]{:S(2)}) copy-start(f32[768]{0:T(1024)} %get-tuple-element.183) | copy-start | bytes 9220
  429.2 21.3 %copy-start.38 = (f32[768]{0:T(1024)S(1)}, f32[768]{0:T(1024)}, u32[]{:S(2)}) copy-start(f32[768]{0:T(1024)} %get-tuple-element.182) | copy-start | bytes 9220
  430.6 38.8 %copy-start.7 = (bf16[256,768]{1,0:T(8,128)(2,1)S(1)}, bf16[256,768]{1,0:T(8,128)(2,1)}, u32[]{:S(2)}) copy-start(bf16[256,768]{1,0:T(8,128)(2,1)} %param.21) | copy-start | bytes 1179652
  471.3 56.7 %copy-start.32 = (f32[768]{0:T(1024)S(1)}, f32[768]{0:T(1024)}, u32[]{:S(2)}) copy-start(f32[768]{0:T(1024)} %get-tuple-element.193) | copy-start | bytes 9220
  471.3 56.7 %copy-start.33 = (f32[768]{0:T(1024)S(1)}, f32[768]{0:T(1024)}, u32[]{:S(2)}) copy-start(f32[768]{0:T(1024)} %get-tuple-element.196) | copy-start | bytes 9220
  471.3 56.7 %copy-start.34 = (f32[768]{0:T(1024)S(1)}, f32[768]{0:T(1024)}, u32[]{:S(2)}) copy-start(f32[768]{0:T(1024)} %get-tuple-element.286) | copy-start | bytes 9220
  471.3 56.7 %copy-start.35 = (f32[768]{0:T(1024)S(1)}, f32[768]{0:T(1024)}, u32[]{:S(2)}) copy-start(f32[768]{0:T(1024)} %get-tuple-element.126) | copy-start | bytes 9220
  471.3 56.7 %copy-start.36 = (f32[768]{0:T(1024)S(1)}, f32[768]{0:T(1024)}, u32[]{:S(2)}) copy-start(f32[768]{0:T(1024)} %get-tuple-element.195) | copy-start | bytes 9220
  471.4 56.7 %copy-start.37 = (f32[768]{0:T(1024)S(1)}, f32[768]{0:T(1024)}, u32[]{:S(2)}) copy-start(f32[768]{0:T(1024)} %get-tuple-element.288) | copy-start | bytes 9220
  471.4 125.1 %copy-start.3 = (f32[256,768]{1,0:T(8,128)S(1)}, f32[256,768]{1,0:T(8,128)}, u32[]{:S(2)}) copy-start(f32[256,768]{1,0:T(8,128)} %copy-done.2) | copy-start | bytes 2359300
  471.4 125.1 %copy-start.115 = (f32[256]{0:T(256)S(1)}, f32[256]{0:T(256)}, u32[]{:S(2)}) copy-start(f32[256]{0:T(256)} %copy-done.114) | copy-start | bytes 3076
  (106 other events, 1160.3 us)
Sparse Core Ops, SparseCore 0:
  83.7 65.6 all-gather.2
  165.7 76.4 reduce-scatter.2
  249.5 62.4 all-gather.4
  324.0 76.5 reduce-scatter.4
  403.6 120.0 all-reduce.10
  529.7 157.4 all-reduce.8
where the time goes:
time: 710 us; the launch traced here: 701 us
  waiting for transfers between devices  369 us (52%)
  blocking collectives  97 us (14%)
  matrix products  88.4 us (12%)
  other arithmetic  70.4 us (10%)
  local copies, waits for them, and re-layouts  48.2 us (7%)
  between operations  16.4 us (2%)
  starting transfers between devices  11.6 us (2%)
    psum x1, waiting for transfers between devices, body(): lax.psum((grad_w_value, grad_b_value, grad_kernel, grad_w_out, grad_b_out...  89.3 us
    reduce_scatter x1, waiting for transfers between devices, body(): lax.psum_scatter(jnp.dot(active, w_down, preferred_element_type=jnp.float...  72.7 us
    reduce_scatter x1, waiting for transfers between devices, body(): lax.psum_scatter(dot_last(upper_grad, w_up).astype(jnp.bfloat16), 'tensor...  69.1 us
    psum x1, blocking collectives, body(): lax.psum((grad_w_value, grad_b_value, grad_kernel, grad_w_out, grad_b_out...  68.4 us
    all_gather x1, waiting for transfers between devices, body(): grad_rows_all = lax.all_gather(branch_grad, 'tensor', axis=0, tiled=True)  62.5 us
    dot_general x16, matrix products, dot_last(): lax.dot_general(former, latter, (((1,), (1,)), ((), ())), preferred_eleme...  56.4 us
    all_gather x1, waiting for transfers between devices, body(): gathered = lax.all_gather(first_low, 'tensor', axis=0, tiled=True)  53.2 us
    psum x1, blocking collectives, body(): lax.psum(grad_b_up.astype(jnp.bfloat16), 'dp').astype(jnp.float32)  28.5 us
  transfers between devices with their start and end apart: 6, of which 6 were waited for; matrix products, arithmetic and copies ran while one was open for 12% of the time, Pallas kernels for 0%

commit v1 on v0

--- a/solution.py
+++ b/solution.py
@@ -208,19 +208,22 @@
         grad_gain_ffn,
         grad_shift_ffn,
     ) = lax.psum(
-        (
-            grad_w_value,
-            grad_b_value,
-            grad_kernel,
-            grad_w_out,
-            grad_b_out,
-            grad_gain_attn,
-            grad_shift_attn,
-            grad_b_down,
-            grad_gain_ffn,
-            grad_shift_ffn,
+        lax.psum(
+            (
+                grad_w_value,
+                grad_b_value,
+                grad_kernel,
+                grad_w_out,
+                grad_b_out,
+                grad_gain_attn,
+                grad_shift_attn,
+                grad_b_down,
+                grad_gain_ffn,
+                grad_shift_ffn,
+            ),
+            "dp",
         ),
-        ("dp", "tensor"),
+        "tensor",
     )
     return (
         block_output.astype(jnp.bfloat16),

time: 710 us -> 902 us (1.27)
  waiting for transfers between devices: 369 us -> 523 us
  blocking collectives: 97 us -> 123 us
  local copies, waits for them, and re-layouts: 48.2 us -> 70.4 us
  starting transfers between devices: 11.6 us -> 1.14 us
    psum x1, waiting for transfers between devices: 22.6 us -> 96.7 us  [body(): lax.psum(grad_w_up.astype(jnp.bfloat16), 'dp').astype(jnp.float32)]
    psum x0 -> x1, blocking collectives: none -> 40.2 us  [body(): lax.psum(lax.psum((grad_w_value, grad_b_value, grad_kernel, grad_w_out, g...]
    psum x1, waiting for transfers between devices: 89.3 us -> 124 us  [body(): lax.psum((grad_w_value, grad_b_value, grad_kernel, grad_w_out, grad_b_out...]
    psum x0 -> x1, waiting for transfers between devices: none -> 26.6 us  [body(): lax.psum(lax.psum((grad_w_value, grad_b_value, grad_kernel, grad_w_out, g...]
    another operation x66, local copies, waits for them, and re-layouts: 25 us -> 48 us  [conv_back(): return (value_grad, jnp.stack(tap_rows, axis=0))]
    psum x1, blocking collectives: 68.4 us -> 55.1 us  [body(): lax.psum((grad_w_value, grad_b_value, grad_kernel, grad_w_out, grad_b_out...]
    all_gather x1, waiting for transfers between devices: 53.2 us -> 64 us  [body(): gathered = lax.all_gather(first_low, 'tensor', axis=0, tiled=True)]
    reduce_scatter x1, starting transfers between devices: 11.4 us -> 0.51 us  [body(): lax.psum_scatter(jnp.dot(active, w_down, preferred_element_type=jnp.float...]
  transfers between devices with their start and end apart: 6 -> 7, of which waited for: 6 -> 7; matrix products, arithmetic and copies ran while one was open for 12% -> 2% of each run, Pallas kernels for 0% -> 0%
where the time goes in v1:
time: 902 us; the launch traced here: 892 us
  waiting for transfers between devices  523 us (58%)
  blocking collectives  123 us (14%)
  matrix products  88.3 us (10%)
  other arithmetic  70.7 us (8%)
  local copies, waits for them, and re-layouts  70.4 us (8%)
  between operations  15.4 us (2%)
    psum x1, waiting for transfers between devices, body(): lax.psum((grad_w_value, grad_b_value, grad_kernel, grad_w_out, grad_b_out...  124 us
    psum x1, waiting for transfers between devices, body(): lax.psum(grad_w_up.astype(jnp.bfloat16), 'dp').astype(jnp.float32)  96.7 us
    reduce_scatter x1, waiting for transfers between devices, body(): lax.psum_scatter(dot_last(upper_grad, w_up).astype(jnp.bfloat16), 'tensor...  76.5 us
    reduce_scatter x1, waiting for transfers between devices, body(): lax.psum_scatter(jnp.dot(active, w_down, preferred_element_type=jnp.float...  72.7 us
    all_gather x1, waiting for transfers between devices, body(): gathered = lax.all_gather(first_low, 'tensor', axis=0, tiled=True)  64 us
    all_gather x1, waiting for transfers between devices, body(): grad_rows_all = lax.all_gather(branch_grad, 'tensor', axis=0, tiled=True)  62.5 us
    dot_general x16, matrix products, dot_last(): lax.dot_general(former, latter, (((1,), (1,)), ((), ())), preferred_eleme...  56.4 us
    psum x1, blocking collectives, body(): lax.psum((grad_w_value, grad_b_value, grad_kernel, grad_w_out, grad_b_out...  55.1 us
  transfers between devices with their start and end apart: 7, of which 7 were waited for; matrix products, arithmetic and copies ran while one was open for 2% of the time, Pallas kernels for 0%

profile of v1, /device:TPU:1, one launch (start us, length us, event | category | flops | bytes accessed | tf_op | source)
XLA Modules:
  0.0 892.1 jit_solution(2533941319769814438)
XLA Ops:
  17.3 43.1 %while.12 = (s32[]{:T(128)}, bf16[12,256,256]{2,1,0:T(8,128)(2,1)}, s32[12,256,32]{1,2,0:T(8,128)S(1)}, s32[12,256,32]{1,2,0:T(8,128)S(1)}, s32[256]{0:T(256)S(1)}, /*index=5*/s32[]{:T(128)}) while((s32[]{:T(128)}, bf16[12,256,256]{2,1,0:T(8,128)(2,1)}, s32[12,256,32]{1,2,0:T(8,128)S(1)}, s32[12,256,32]{1,2,0:T(8,128)S(1)}, ...), condition=%wide.region_3.4_spmd.clone.clone, body=%wide.region_2.3_spmd.clone.clone.sunk | while | flops 1078198272 | bytes 330313 | solution.py:125
  17.4 3.6 fusion.266
  24.5 3.6 fusion.266
  28.1 3.6 fusion.266
  35.3 3.6 fusion.266
  42.5 3.6 fusion.266
  49.7 3.6 fusion.266
  53.2 3.6 fusion.266
  66.3 11.6 %add_convert_fusion.2 = bf16[256,768]{1,0:T(8,128)(2,1)S(1)} fusion(f32[256,768]{1,0:T(8,128)S(1)} %copy.51, f32[256,768]{1,0:T(8,128)S(1)} %get-tuple-element.378, f32[768]{0:T(1024)} %get-tuple-element.198, f32[256]{0:T(256)} %get-tuple-element.376, f32[768]{0:T(1024)} %get-tuple-element.199, f32[256]{0:T(256)} %get-tuple-element.375, ...), kind=kLoop, calls=%fused_computation.456 | loop fusion | flops 38338560 | bytes 2231296 | tf_op jit(solution)/shard_map/convert_element_type | solution.py:140
  85.4 64.0 %all-gather.3.cloned.1.call-done = bf16[2048,768]{1,0:T(8,128)(2,1)} async-done(((bf16[256,768]{1,0:T(8,128)(2,1)}), bf16[2048,768]{1,0:T(8,128)(2,1)}) %all-gather.3.cloned.1.call-update) | async-done | bytes 3145744 | tf_op jit(solution)/shard_map/all_gather | solution.py:151
  149.4 11.5 %multiply_convert_fusion = (bf16[2048,384]{1,0:T(8,128)(2,1)S(1)}, f32[2048,384]{1,0:T(8,128)}, f32[2048,384]{1,0:T(8,128)}) fusion(f32[384]{0:T(512)} %convert_element_type.529, bf16[2048,768]{1,0:T(8,128)(2,1)} %all-gather.3.cloned.1.call-done, bf16[768,384]{1,0:T(8,128)(2,1)} %param.29), kind=kOutput, calls=%fused_computation.148 | convolution fusion | flops 1259864064 | bytes 11601408 | tf_op jit(solution)/shard_map/dot_general | solution.py:152
  169.5 72.7 %reduce-scatter.3.cloned.1.call-done = bf16[256,768]{1,0:T(8,128)(2,1)} async-done(((bf16[2048,768]{1,0:T(8,128)(2,1)}), bf16[256,768]{1,0:T(8,128)(2,1)}) %reduce-scatter.3.cloned.1.call-update) | async-done | bytes 393232 | tf_op jit(solution)/shard_map/reduce_scatter | solution.py:155
  249.4 62.5 %all-gather.5.cloned.1.call-done = bf16[2048,768]{1,0:T(8,128)(2,1)} async-done(((bf16[256,768]{1,0:T(8,128)(2,1)}), bf16[2048,768]{1,0:T(8,128)(2,1)}) %all-gather.5.cloned.1.call-update) | async-done | bytes 3145744 | tf_op jit(solution)/shard_map/all_gather | solution.py:167
  311.9 7.3 fusion.230
  324.2 76.5 %reduce-scatter.5.cloned.1.call-done = bf16[256,768]{1,0:T(8,128)(2,1)} async-done(((bf16[2048,768]{1,0:T(8,128)(2,1)}), bf16[256,768]{1,0:T(8,128)(2,1)}) %reduce-scatter.5.cloned.1.call-update) | async-done | bytes 393232 | tf_op jit(solution)/shard_map/reduce_scatter | solution.py:173
  431.6 12.1 %convert_reduce_fusion.3 = (f32[768]{0:T(1024)S(1)}, bf16[256,768]{1,0:T(8,128)(2,1)S(1)}) fusion(f32[256]{0:T(256)} %copy-done.76, f32[256,768]{1,0:T(8,128)S(1)} %copy.53, f32[768]{0:T(1024)} %get-tuple-element.198, f32[256]{0:T(256)} %get-tuple-element.313, f32[768]{0:T(1024)} %get-tuple-element.199, f32[256]{0:T(256)} %get-tuple-element.331, ...), kind=kLoop, calls=%fused_computation.446 | loop fusion | flops 38927616 | bytes 2235392 | tf_op jit(solution)/shard_map/reduce_sum | solution.py:191
  487.9 5.8 stack.263
  494.0 4.7 convolution_convert_fusion.2
  501.4 123.5 %all-reduce.12.cloned.1.call-done = (f32[768,768]{0,1:T(8,128)}, f32[65,768]{1,0:T(8,128)}, f32[768,768]{1,0:T(8,128)}) async-done(((f32[768,768]{0,1:T(8,128)}, f32[65,768]{1,0:T(8,128)}, f32[768,768]{1,0:T(8,128)}), (f32[768,768]{0,1:T(8,128)}, f32[65,768]{1,0:T(8,128)}, f32[768,768]{1,0:T(8,128)})) %all-reduce.12.cloned.1.call-update) | async-done | bytes 4918288 | tf_op jit(solution)/shard_map/psum | solution.py:211
  625.0 28.0 %psum.176 = bf16[384]{0:T(512)(128)(2,1)S(1)} all-reduce(bf16[384]{0:T(512)(128)(2,1)S(1)} %copy-done.86), channel_id=1, replica_groups=mesh['dp'=16,'tensor'=8] {'dp'}, use_global_device_ids=true, to_apply=%region_101.102 | all-reduce | flops 384 | bytes 1536 | tf_op jit(solution)/shard_map/psum | solution.py:197
  653.6 96.7 %all-reduce.16.cloned.1.call-done = (bf16[768,384]{1,0:T(8,128)(2,1)}, bf16[384,768]{1,0:T(8,128)(2,1)}) async-done(((bf16[768,384]{1,0:T(8,128)(2,1)}, bf16[384,768]{1,0:T(8,128)(2,1)}), (bf16[768,384]{1,0:T(8,128)(2,1)}, bf16[384,768]{1,0:T(8,128)(2,1)})) %all-reduce.16.cloned.1.call-update) | async-done | bytes 1179664 | tf_op jit(solution)/shard_map/psum | solution.py:195
  754.7 55.1 %all-reduce.3 = (f32[768]{0:T(1024)S(1)}, f32[768]{0:T(1024)S(1)}, f32[768]{0:T(1024)S(1)}, f32[768]{0:T(1024)S(1)}, f32[768]{0:T(1024)S(1)}, /*index=5*/f32[768]{0:T(1024)S(1)}, f32[768]{0:T(1024)S(1)}) all-reduce(f32[768]{0:T(1024)S(1)} %get-tuple-element.300, f32[768]{0:T(1024)S(1)} %copy-done.37, ...), channel_id=1, replica_groups=mesh['dp'=16,'tensor'=8] {'dp'}, use_global_device_ids=true, to_apply=%region_19.20 | all-reduce | flops 5376 | bytes 43008 | tf_op jit(solution)/shard_map/psum | solution.py:211
  809.9 40.2 %all-reduce.5 = (f32[768]{0:T(1024)}, f32[768]{0:T(1024)}, f32[768]{0:T(1024)}, f32[768]{0:T(1024)}, f32[768]{0:T(1024)}, /*index=5*/f32[768]{0:T(1024)}, f32[768]{0:T(1024)}) all-reduce(f32[768]{0:T(1024)S(1)} %get-tuple-element.272, f32[768]{0:T(1024)S(1)} %get-tuple-element.273, ...), channel_id=1, replica_groups=mesh['dp'=16,'tensor'=8] {'tensor'}, use_global_device_ids=true, to_apply=%region_20.21 | all-reduce | flops 5376 | bytes 43008 | tf_op jit(solution)/shard_map/psum | solution.py:210
  851.4 26.6 %all-reduce.14.cloned.1.call-done = (f32[768,768]{0,1:T(8,128)}, f32[65,768]{1,0:T(8,128)}, f32[768,768]{1,0:T(8,128)}) async-done(((f32[768,768]{0,1:T(8,128)}, f32[65,768]{1,0:T(8,128)}, f32[768,768]{1,0:T(8,128)}), (f32[768,768]{0,1:T(8,128)}, f32[65,768]{1,0:T(8,128)}, f32[768,768]{1,0:T(8,128)})) %all-reduce.14.cloned.1.call-update) | async-done | bytes 4918288 | tf_op jit(solution)/shard_map/psum | solution.py:210
  (349 shorter events, 152.5 us)
Async XLA Ops:
  7.2 53.3 %copy-start = (bf16[768,768]{1,0:T(8,128)(2,1)S(1)}, bf16[768,768]{1,0:T(8,128)(2,1)}, u32[]{:S(2)}) copy-start(bf16[768,768]{1,0:T(8,128)(2,1)} %param.22) | copy-start | bytes 3538948
  7.2 142.2 %all-gather.3.cloned.1.call-start = ((), (), s32[]{:S(2)}) async-start(), calls=%async_computation.2 | async-start | bytes 3538944 | tf_op jit(solution)/shard_map/all_gather | solution.py:151
  17.3 43.1 %copy-start.85 = (s32[256]{0:T(256)S(1)}, s32[256]{0:T(256)}, u32[]{:S(2)}) copy-start(s32[256]{0:T(256)} %param.37) | copy-start | bytes 3076
  17.3 43.1 %copy-start.82 = (bf16[768]{0:T(1024)(128)(2,1)S(1)}, bf16[768]{0:T(1024)(128)(2,1)}, u32[]{:S(2)}) copy-start(bf16[768]{0:T(1024)(128)(2,1)} %param.23) | copy-start | bytes 4612
  17.3 43.1 %copy-start.6 = (bf16[256,768]{1,0:T(8,128)(2,1)S(1)}, bf16[256,768]{1,0:T(8,128)(2,1)}, u32[]{:S(2)}) copy-start(bf16[256,768]{1,0:T(8,128)(2,1)} %param.21) | copy-start | bytes 1179652
  83.6 158.7 %reduce-scatter.3.cloned.1.call-start = ((), (), s32[]{:S(2)}) async-start(), calls=%async_computation.3 | async-start | bytes 3538944 | tf_op jit(solution)/shard_map/reduce_scatter | solution.py:155
  165.6 146.3 %all-gather.5.cloned.1.call-start = ((), (), s32[]{:S(2)}) async-start(), calls=%async_computation.4 | async-start | bytes 3538944 | tf_op jit(solution)/shard_map/all_gather | solution.py:167
  249.4 151.3 %reduce-scatter.5.cloned.1.call-start = ((), (), s32[]{:S(2)}) async-start(), calls=%async_computation.5 | async-start | bytes 3538944 | tf_op jit(solution)/shard_map/reduce_scatter | solution.py:173
  323.9 301.0 %all-reduce.12.cloned.1.call-start = ((), (), s32[]{:S(2)}) async-start(), calls=%async_computation.6 | async-start | bytes 9879552 | tf_op jit(solution)/shard_map/psum | solution.py:211
  430.1 54.4 %copy-start.40 = (f32[768]{0:T(1024)S(1)}, f32[768]{0:T(1024)}, u32[]{:S(2)}) copy-start(f32[768]{0:T(1024)} %get-tuple-element.184) | copy-start | bytes 9220
  430.1 54.4 %copy-start.39 = (f32[768]{0:T(1024)S(1)}, f32[768]{0:T(1024)}, u32[]{:S(2)}) copy-start(f32[768]{0:T(1024)} %get-tuple-element.183) | copy-start | bytes 9220
  430.1 54.5 %copy-start.38 = (f32[768]{0:T(1024)S(1)}, f32[768]{0:T(1024)}, u32[]{:S(2)}) copy-start(f32[768]{0:T(1024)} %get-tuple-element.182) | copy-start | bytes 9220
  430.1 55.8 %copy-start.7 = (bf16[256,768]{1,0:T(8,128)(2,1)S(1)}, bf16[256,768]{1,0:T(8,128)(2,1)}, u32[]{:S(2)}) copy-start(bf16[256,768]{1,0:T(8,128)(2,1)} %param.21) | copy-start | bytes 1179652
  493.7 256.7 %all-reduce.16.cloned.1.call-start = ((), (), s32[]{:S(2)}) async-start(), calls=%async_computation.8 | async-start | bytes 2359296 | tf_op jit(solution)/shard_map/psum | solution.py:195
  501.4 123.7 %copy-start.86 = (bf16[384]{0:T(512)(128)(2,1)S(1)}, bf16[384]{0:T(512)(128)(2,1)}, u32[]{:S(2)}) copy-start(bf16[384]{0:T(512)(128)(2,1)} %get-tuple-element.294) | copy-start | bytes 2308
  501.4 376.6 %all-reduce.14.cloned.1.call-start = ((), (), s32[]{:S(2)}) async-start(), calls=%async_computation.7 | async-start | bytes 9879552 | tf_op jit(solution)/shard_map/psum | solution.py:210
  625.0 129.7 %copy-start.32 = (f32[768]{0:T(1024)S(1)}, f32[768]{0:T(1024)}, u32[]{:S(2)}) copy-start(f32[768]{0:T(1024)} %get-tuple-element.193) | copy-start | bytes 9220
  625.0 129.7 %copy-start.33 = (f32[768]{0:T(1024)S(1)}, f32[768]{0:T(1024)}, u32[]{:S(2)}) copy-start(f32[768]{0:T(1024)} %get-tuple-element.196) | copy-start | bytes 9220
  625.0 129.7 %copy-start.34 = (f32[768]{0:T(1024)S(1)}, f32[768]{0:T(1024)}, u32[]{:S(2)}) copy-start(f32[768]{0:T(1024)} %get-tuple-element.296) | copy-start | bytes 9220
  625.0 129.7 %copy-start.35 = (f32[768]{0:T(1024)S(1)}, f32[768]{0:T(1024)}, u32[]{:S(2)}) copy-start(f32[768]{0:T(1024)} %get-tuple-element.126) | copy-start | bytes 9220
  625.0 129.7 %copy-start.36 = (f32[768]{0:T(1024)S(1)}, f32[768]{0:T(1024)}, u32[]{:S(2)}) copy-start(f32[768]{0:T(1024)} %get-tuple-element.195) | copy-start | bytes 9220
  625.0 129.7 %copy-start.37 = (f32[768]{0:T(1024)S(1)}, f32[768]{0:T(1024)}, u32[]{:S(2)}) copy-start(f32[768]{0:T(1024)} %get-tuple-element.298) | copy-start | bytes 9220
  625.0 225.1 %copy-start.3 = (f32[256,768]{1,0:T(8,128)S(1)}, f32[256,768]{1,0:T(8,128)}, u32[]{:S(2)}) copy-start(f32[256,768]{1,0:T(8,128)} %copy-done.2) | copy-start | bytes 2359300
  625.0 225.1 %copy-start.81 = (f32[256]{0:T(256)S(1)}, f32[256]{0:T(256)}, u32[]{:S(2)}) copy-start(f32[256]{0:T(256)} %copy-done.80) | copy-start | bytes 3076
  (73 other events, 482.8 us)
Sparse Core Ops, SparseCore 0:
  83.7 65.6 all-gather.2
  165.8 76.4 reduce-scatter.2
  249.5 62.4 all-gather.4
  324.1 76.5 reduce-scatter.4
  493.8 131.1 all-reduce.11
  628.7 121.6 all-reduce.15
  753.4 124.6 all-reduce.13
